TPU v7x, 32 devices: a whole 2x2x4 slice. The times are simulated.
32 devices in a mesh: gx: 4 (over z), gy: 8 (over y, x, core).
Axes of the slice: x: 2, y: 2, z: 4, core: 2. Of those that a mesh axis runs over, the one named last changes fastest.
Arguments:
- features: bfloat16 [8192, 512], P(('gx', 'gy')), may hold values from -6 to 6
- cotangent: bfloat16 [8192, 512], P(('gx', 'gy')), may hold values from -6 to 6
- self_weight: bfloat16 [3, 512, 512], replicated, may hold values from -0.25 to 0.25
- neigh_weight: bfloat16 [3, 512, 512], replicated, may hold values from -0.25 to 0.25
- block_val: bfloat16 [64, 4, 128, 128], P(('gx', 'gy')), may hold values from -0.25 to 0.25
- block_col: int32 [64, 4], P(('gx', 'gy')), may hold values from 0 to 5
- send_idx: int32 [32, 32, 16], P(('gx', 'gy')), may hold values from 0 to 255
- send_count: int32 [32, 32], P(('gx', 'gy')), may hold values from 0 to 16, as said below
Outputs:
- self_grad: bfloat16 [3, 512, 512], replicated
- neigh_grad: bfloat16 [3, 512, 512], replicated
- input_grad: bfloat16 [8192, 512], P(('gx', 'gy'))
Inputs may be any that keep to these rules, and one draw needn't show every extreme that they name: `send_count`: at most 16 rows from one device to one peer; in every draw some receivers get exactly 16 from every device.
All inputs are finite; a program needn't handle non-finite values.
Results may differ from a plain program's by a relative error of at most 0.02.
Values may be sent and summed in bfloat16 or wider, within the bound.
No kernel may reach another device: no remote copies, remote signals or barrier semaphores. Data moves between devices by JAX's collectives and lax.ppermute only.
A program may use at most 128 MiB of HBM per device.

v0:
```python
import math
import jax
import jax.numpy as jnp
from jax import lax
from jax.sharding import PartitionSpec as P


def gather_sum(extended, values, columns, tile):
    width = extended.shape[1]
    tiled = extended.reshape(-1, tile, width)[columns]
    total = jnp.einsum("rbij,rbjd->rid", values, tiled, preferred_element_type=jnp.float32)
    return total.reshape(-1, width)


def spread_back(upstream, values, columns, ext_tiles, tile):
    width = upstream.shape[1]
    contrib = jnp.einsum(
        "rbij,rid->rbjd",
        values,
        upstream.reshape(-1, tile, width),
        preferred_element_type=jnp.float32,
    )
    onehot = (
        columns.reshape(-1)[None, :] == jnp.arange(ext_tiles, dtype=jnp.int32)[:, None]
    ).astype(jnp.float32)
    total = jnp.einsum(
        "cn,njd->cjd", onehot, contrib.reshape(-1, tile, width), precision=lax.Precision.HIGHEST
    )
    return total.reshape(-1, width)


def per_device(
    features, cotangent, self_weight, neigh_weight, block_val, block_col, send_idx, send_count
):
    outer = lax.axis_size("gx")
    inner = lax.axis_size("gy")
    devices = outer * inner
    node_rows, width = features.shape
    tile = block_val.shape[2]
    layers = self_weight.shape[0]
    slots = send_idx.shape[2]
    halo_rows = devices * slots
    ext_tiles = (node_rows + halo_rows) // tile
    scale = 1.0 / math.sqrt(node_rows * devices)
    row_ids = send_idx.reshape(-1)
    live = (jnp.arange(slots, dtype=jnp.int32)[None, :] < send_count.reshape(-1)[:, None]).reshape(
        -1, 1
    )
    hiddens = [features]
    aggregates = []
    preacts = []
    hidden = features
    for layer_at in range(layers):
        picked = jnp.where(live, jnp.take(hidden, row_ids, axis=0), jnp.zeros((), hidden.dtype))
        picked = picked.reshape(outer, inner, slots, width)
        send_arrived = lax.all_to_all(
            lax.all_to_all(picked, "gx", split_axis=0, concat_axis=0, tiled=True),
            "gy",
            split_axis=1,
            concat_axis=1,
            tiled=True,
        )
        extended = jnp.concatenate([hidden, send_arrived.reshape(halo_rows, width)], axis=0)
        aggregate = gather_sum(extended, block_val, block_col, tile).astype(jnp.bfloat16)
        preact = jnp.dot(
            hidden, self_weight[layer_at], preferred_element_type=jnp.float32
        ) + jnp.dot(aggregate, neigh_weight[layer_at], preferred_element_type=jnp.float32)
        aggregates.append(aggregate)
        preacts.append(preact)
        if layer_at < layers - 1:
            hidden = jax.nn.silu(preact).astype(jnp.bfloat16)
            hiddens.append(hidden)
    transposed = (((0,), (0,)), ((), ()))
    against = (((1,), (1,)), ((), ()))
    self_list = [None] * layers
    neigh_list = [None] * layers
    grad = cotangent
    for layer_at in reversed(range(layers)):
        preact = preacts[layer_at]
        sigma = jax.nn.sigmoid(preact)
        delta = (grad.astype(jnp.float32) * sigma * (1.0 + preact * (1.0 - sigma))).astype(
            jnp.bfloat16
        )
        self_term = lax.dot_general(
            hiddens[layer_at], delta, transposed, preferred_element_type=jnp.float32
        )
        neigh_term = lax.dot_general(
            aggregates[layer_at], delta, transposed, preferred_element_type=jnp.float32
        )
        self_sum, neigh_sum = lax.psum((self_term, neigh_term), ("gx", "gy"))
        self_list[layer_at] = (self_sum * scale).astype(jnp.bfloat16)
        neigh_list[layer_at] = (neigh_sum * scale).astype(jnp.bfloat16)
        own_part = lax.dot_general(
            delta, self_weight[layer_at], against, preferred_element_type=jnp.float32
        )
        upstream = lax.dot_general(
            delta, neigh_weight[layer_at], against, preferred_element_type=jnp.float32
        ).astype(jnp.bfloat16)
        ext_grad = spread_back(upstream, block_val, block_col, ext_tiles, tile)
        outgoing = ext_grad[node_rows:].astype(jnp.bfloat16).reshape(outer, inner, slots, width)
        arrived = lax.all_to_all(
            lax.all_to_all(outgoing, "gx", split_axis=0, concat_axis=0, tiled=True),
            "gy",
            split_axis=1,
            concat_axis=1,
            tiled=True,
        )
        masked = jnp.where(
            live, arrived.reshape(halo_rows, width).astype(jnp.float32), jnp.zeros((), jnp.float32)
        )
        returned = jnp.zeros((node_rows, width), jnp.float32).at[row_ids].add(masked)
        grad = (own_part + ext_grad[:node_rows] + returned).astype(jnp.bfloat16)
    self_grad = jnp.stack(self_list)
    neigh_grad = jnp.stack(neigh_list)
    return (self_grad, neigh_grad, grad)


def solution(mesh):
    return jax.shard_map(
        per_device,
        mesh=mesh,
        in_specs=(
            P(("gx", "gy"), None),
            P(("gx", "gy"), None),
            P(),
            P(),
            P(("gx", "gy"), None, None, None),
            P(("gx", "gy"), None),
            P(("gx", "gy"), None, None),
            P(("gx", "gy"), None),
        ),
        out_specs=(P(), P(), P(("gx", "gy"), None)),
        check_vma=False,
    )
```

profile of v0, /device:TPU:0, one launch (start us, length us, event | category | flops | bytes accessed | tf_op | source)
XLA Modules:
  0.0 399.9 jit_solution(2928996028955188981)
XLA Ops:
  12.1 20.8 %all_to_all.60 = bf16[4,8,16,512]{3,2,1,0:T(8,128)(2,1)S(1)} all-to-all(bf16[4,8,16,512]{3,2,1,0:T(8,128)(2,1)S(1)} %bitcast.184), channel_id=1, replica_groups=mesh['gx'=4,'gy'=8] {'gx'}, dimensions={0} | all-to-all | bytes 1048576 | tf_op jit(solution)/shard_map/all_to_all | solution.py:57
  33.7 3.7 all-to-all-start.1
  38.7 8.5 %all-to-all-done.1 = bf16[4,8,16,512]{3,2,0,1:T(8,128)(2,1)S(1)} async-done(((bf16[4,8,16,512]{3,2,0,1:T(8,128)(2,1)}), bf16[4,8,16,512]{3,2,0,1:T(8,128)(2,1)S(1)}, u32[]{:S(2)}, u32[]{:S(2)}) %all-to-all-start.1) | async-done | bytes 524320 | tf_op jit(solution)/shard_map/all_to_all | solution.py:56
  54.9 14.9 %all_to_all.61 = bf16[4,8,16,512]{3,2,1,0:T(8,128)(2,1)S(1)} all-to-all(bf16[4,8,16,512]{3,2,1,0:T(8,128)(2,1)S(1)} %bitcast.185), channel_id=1, replica_groups=mesh['gx'=4,'gy'=8] {'gx'}, dimensions={0} | all-to-all | bytes 1048576 | tf_op jit(solution)/shard_map/all_to_all | solution.py:57
  70.7 4.3 %all-to-all-start.3 = ((bf16[4,8,16,512]{3,2,0,1:T(8,128)(2,1)}), bf16[4,8,16,512]{3,2,0,1:T(8,128)(2,1)S(1)}, u32[]{:S(2)}, u32[]{:S(2)}) async-start(bf16[4,8,16,512]{3,2,0,1:T(8,128)(2,1)} %copy.111), calls=%async_computation.3 | async-start | bytes 1048576 | tf_op jit(solution)/shard_map/all_to_all | solution.py:56
  76.1 8.6 %all-to-all-done.3 = bf16[4,8,16,512]{3,2,0,1:T(8,128)(2,1)S(1)} async-done(((bf16[4,8,16,512]{3,2,0,1:T(8,128)(2,1)}), bf16[4,8,16,512]{3,2,0,1:T(8,128)(2,1)S(1)}, u32[]{:S(2)}, u32[]{:S(2)}) %all-to-all-start.3) | async-done | bytes 524320 | tf_op jit(solution)/shard_map/all_to_all | solution.py:56
  92.4 14.9 %all_to_all.62 = bf16[4,8,16,512]{3,2,1,0:T(8,128)(2,1)S(1)} all-to-all(bf16[4,8,16,512]{3,2,1,0:T(8,128)(2,1)S(1)} %bitcast.183), channel_id=1, replica_groups=mesh['gx'=4,'gy'=8] {'gx'}, dimensions={0} | all-to-all | bytes 1048576 | tf_op jit(solution)/shard_map/all_to_all | solution.py:57
  108.2 4.3 %all-to-all-start.5 = ((bf16[4,8,16,512]{3,2,0,1:T(8,128)(2,1)}), bf16[4,8,16,512]{3,2,0,1:T(8,128)(2,1)S(1)}, u32[]{:S(2)}, u32[]{:S(2)}) async-start(bf16[4,8,16,512]{3,2,0,1:T(8,128)(2,1)} %copy.113), calls=%async_computation.5 | async-start | bytes 1048576 | tf_op jit(solution)/shard_map/all_to_all | solution.py:56
  113.7 8.5 %all-to-all-done.5 = bf16[4,8,16,512]{3,2,0,1:T(8,128)(2,1)S(1)} async-done(((bf16[4,8,16,512]{3,2,0,1:T(8,128)(2,1)}), bf16[4,8,16,512]{3,2,0,1:T(8,128)(2,1)S(1)}, u32[]{:S(2)}, u32[]{:S(2)}) %all-to-all-start.5) | async-done | bytes 524320 | tf_op jit(solution)/shard_map/all_to_all | solution.py:56
  133.5 4.1 %all-to-all-start.6 = ((bf16[4,8,16,512]{3,2,1,0:T(8,128)(2,1)}), bf16[4,8,16,512]{3,2,1,0:T(8,128)(2,1)}, u32[]{:S(2)}, u32[]{:S(2)}) async-start(bf16[4,8,16,512]{3,2,1,0:T(8,128)(2,1)} %copy.119), calls=%async_computation.6 | async-start | bytes 1048576 | tf_op jit(solution)/shard_map/all_to_all | solution.py:102
  137.7 12.5 %all-to-all-done.6 = bf16[4,8,16,512]{3,2,1,0:T(8,128)(2,1)} async-done(((bf16[4,8,16,512]{3,2,1,0:T(8,128)(2,1)}), bf16[4,8,16,512]{3,2,1,0:T(8,128)(2,1)}, u32[]{:S(2)}, u32[]{:S(2)}) %all-to-all-start.6) | async-done | bytes 524320 | tf_op jit(solution)/shard_map/all_to_all | solution.py:102
  152.1 4.3 %all-to-all-start.7 = ((bf16[4,8,16,512]{3,2,0,1:T(8,128)(2,1)}), bf16[4,8,16,512]{3,2,0,1:T(8,128)(2,1)}, u32[]{:S(2)}, u32[]{:S(2)}) async-start(bf16[4,8,16,512]{3,2,0,1:T(8,128)(2,1)} %copy.120), calls=%async_computation.7 | async-start | bytes 1048576 | tf_op jit(solution)/shard_map/all_to_all | solution.py:101
  158.1 8.1 %all-to-all-done.7 = bf16[4,8,16,512]{3,2,0,1:T(8,128)(2,1)} async-done(((bf16[4,8,16,512]{3,2,0,1:T(8,128)(2,1)}), bf16[4,8,16,512]{3,2,0,1:T(8,128)(2,1)}, u32[]{:S(2)}, u32[]{:S(2)}) %all-to-all-start.7) | async-done | bytes 524320 | tf_op jit(solution)/shard_map/all_to_all | solution.py:101
  167.5 4.0 scatter_fusion
  179.6 4.1 %all-to-all-start.8 = ((bf16[4,8,16,512]{3,2,1,0:T(8,128)(2,1)}), bf16[4,8,16,512]{3,2,1,0:T(8,128)(2,1)}, u32[]{:S(2)}, u32[]{:S(2)}) async-start(bf16[4,8,16,512]{3,2,1,0:T(8,128)(2,1)} %copy.125), calls=%async_computation.8 | async-start | bytes 1048576 | tf_op jit(solution)/shard_map/all_to_all | solution.py:102
  189.1 7.2 %all-to-all-done.8 = bf16[4,8,16,512]{3,2,1,0:T(8,128)(2,1)} async-done(((bf16[4,8,16,512]{3,2,1,0:T(8,128)(2,1)}), bf16[4,8,16,512]{3,2,1,0:T(8,128)(2,1)}, u32[]{:S(2)}, u32[]{:S(2)}) %all-to-all-start.8) | async-done | bytes 524320 | tf_op jit(solution)/shard_map/all_to_all | solution.py:102
  198.2 4.3 %all-to-all-start.9 = ((bf16[4,8,16,512]{3,2,0,1:T(8,128)(2,1)}), bf16[4,8,16,512]{3,2,0,1:T(8,128)(2,1)S(1)}, u32[]{:S(2)}, u32[]{:S(2)}) async-start(bf16[4,8,16,512]{3,2,0,1:T(8,128)(2,1)} %copy.126), calls=%async_computation.9 | async-start | bytes 1048576 | tf_op jit(solution)/shard_map/all_to_all | solution.py:101
  205.2 7.0 %all-to-all-done.9 = bf16[4,8,16,512]{3,2,0,1:T(8,128)(2,1)S(1)} async-done(((bf16[4,8,16,512]{3,2,0,1:T(8,128)(2,1)}), bf16[4,8,16,512]{3,2,0,1:T(8,128)(2,1)S(1)}, u32[]{:S(2)}, u32[]{:S(2)}) %all-to-all-start.9) | async-done | bytes 524320 | tf_op jit(solution)/shard_map/all_to_all | solution.py:101
  212.5 4.0 %scatter_fusion.1 = f32[256,512]{1,0:T(8,128)S(1)} fusion(f32[256,512]{1,0:T(8,128)S(1)} %convolution_add_fusion.1, s32[512]{0:T(512)S(1)} %bitcast.199, f32[512,512]{1,0:T(8,128)S(1)} %bitcast_select_fusion.1), kind=kCustom, calls=%fused_computation.7 | custom fusion | flops 262144 | bytes 3147776 | tf_op jit(solution)/shard_map/scatter-add | solution.py:111
  226.5 22.2 %all_to_all.63 = bf16[4,8,16,512]{3,2,1,0:T(8,128)(2,1)S(1)} all-to-all(bf16[4,8,16,512]{3,2,1,0:T(8,128)(2,1)S(1)} %copy.136), channel_id=1, replica_groups=mesh['gx'=4,'gy'=8] {'gx'}, dimensions={0} | all-to-all | bytes 1048576 | tf_op jit(solution)/shard_map/all_to_all | solution.py:102
  249.5 3.5 all-to-all-start.11
  254.8 7.9 %all-to-all-done.11 = bf16[4,8,16,512]{3,2,0,1:T(8,128)(2,1)S(1)} async-done(((bf16[4,8,16,512]{3,2,0,1:T(8,128)(2,1)}), bf16[4,8,16,512]{3,2,0,1:T(8,128)(2,1)S(1)}, u32[]{:S(2)}, u32[]{:S(2)}) %all-to-all-start.11) | async-done | bytes 524320 | tf_op jit(solution)/shard_map/all_to_all | solution.py:101
  263.0 3.8 scatter_fusion.2
  267.5 117.8 %all-reduce.3.cloned.1.call-done = (f32[512,512]{0,1:T(8,128)}, f32[512,512]{0,1:T(8,128)}, f32[512,512]{0,1:T(8,128)}, f32[512,512]{0,1:T(8,128)}, f32[512,512]{0,1:T(8,128)}, /*index=5*/f32[512,512]{0,1:T(8,128)}) async-done(((f32[512,512]{0,1:T(8,128)}, f32[512,512]{0,1:T(8,128)}, f32[512,512]{0,1:T(8,128)}, f32[512,512]{0,1:T(8,128)}, f32[512,512]{0,1:T(8,128)}, /*index=5*/f32[512,512]{0,1:T(8,128)}), ...) | async-done | bytes 6291472 | tf_op jit(solution)/shard_map/psum | solution.py:90
  (132 shorter events, 81.8 us)
Async XLA Ops:
  7.2 41.7 %copy-start = (bf16[2,4,128,128]{3,2,1,0:T(8,128)(2,1)S(1)}, bf16[2,4,128,128]{3,2,1,0:T(8,128)(2,1)}, u32[]{:S(2)}) copy-start(bf16[2,4,128,128]{3,2,1,0:T(8,128)(2,1)} %param.14) | copy-start | bytes 786436
  12.1 25.4 %copy-start.17 = (s32[2,4]{1,0:T(2,128)S(1)}, s32[2,4]{1,0:T(2,128)}, u32[]{:S(2)}) copy-start(s32[2,4]{1,0:T(2,128)} %param.15) | copy-start | bytes 100
  12.1 25.5 %copy-start.1 = (bf16[256,512]{1,0:T(8,128)(2,1)S(1)}, bf16[256,512]{1,0:T(8,128)(2,1)}, u32[]{:S(2)}) copy-start(bf16[256,512]{1,0:T(8,128)(2,1)} %param.10) | copy-start | bytes 786436
  12.1 25.4 %copy-start.2 = (bf16[3,512,512]{2,1,0:T(8,128)(2,1)S(1)}, bf16[3,512,512]{2,1,0:T(8,128)(2,1)}, u32[]{:S(2)}) copy-start(bf16[3,512,512]{2,1,0:T(8,128)(2,1)} %param.12) | copy-start | bytes 4718596
  33.7 13.4 %all-to-all-start.1 = ((bf16[4,8,16,512]{3,2,0,1:T(8,128)(2,1)}), bf16[4,8,16,512]{3,2,0,1:T(8,128)(2,1)S(1)}, u32[]{:S(2)}, u32[]{:S(2)}) async-start(bf16[4,8,16,512]{3,2,0,1:T(8,128)(2,1)} %copy.109), calls=%async_computation.1 | async-start | bytes 1048576 | tf_op jit(solution)/shard_map/all_to_all | solution.py:56
  50.5 2.3 copy-start.7
  70.7 14.0 %all-to-all-start.3 = ((bf16[4,8,16,512]{3,2,0,1:T(8,128)(2,1)}), bf16[4,8,16,512]{3,2,0,1:T(8,128)(2,1)S(1)}, u32[]{:S(2)}, u32[]{:S(2)}) async-start(bf16[4,8,16,512]{3,2,0,1:T(8,128)(2,1)} %copy.111), calls=%async_computation.3 | async-start | bytes 1048576 | tf_op jit(solution)/shard_map/all_to_all | solution.py:56
  88.0 2.3 copy-start.9
  108.2 14.0 %all-to-all-start.5 = ((bf16[4,8,16,512]{3,2,0,1:T(8,128)(2,1)}), bf16[4,8,16,512]{3,2,0,1:T(8,128)(2,1)S(1)}, u32[]{:S(2)}, u32[]{:S(2)}) async-start(bf16[4,8,16,512]{3,2,0,1:T(8,128)(2,1)} %copy.113), calls=%async_computation.5 | async-start | bytes 1048576 | tf_op jit(solution)/shard_map/all_to_all | solution.py:56
  123.3 2.3 copy-start.11
  125.6 31.2 %copy-start.3 = (bf16[256,512]{1,0:T(8,128)(2,1)}, bf16[256,512]{1,0:T(8,128)(2,1)S(1)}, u32[]{:S(2)}) copy-start(bf16[256,512]{1,0:T(8,128)(2,1)S(1)} %multiply_convert_fusion.8) | copy-start | bytes 786436
  133.5 16.7 %all-to-all-start.6 = ((bf16[4,8,16,512]{3,2,1,0:T(8,128)(2,1)}), bf16[4,8,16,512]{3,2,1,0:T(8,128)(2,1)}, u32[]{:S(2)}, u32[]{:S(2)}) async-start(bf16[4,8,16,512]{3,2,1,0:T(8,128)(2,1)} %copy.119), calls=%async_computation.6 | async-start | bytes 1048576 | tf_op jit(solution)/shard_map/all_to_all | solution.py:102
  152.1 14.1 %all-to-all-start.7 = ((bf16[4,8,16,512]{3,2,0,1:T(8,128)(2,1)}), bf16[4,8,16,512]{3,2,0,1:T(8,128)(2,1)}, u32[]{:S(2)}, u32[]{:S(2)}) async-start(bf16[4,8,16,512]{3,2,0,1:T(8,128)(2,1)} %copy.120), calls=%async_computation.7 | async-start | bytes 1048576 | tf_op jit(solution)/shard_map/all_to_all | solution.py:101
  167.5 4.0 %copy-start.13 = (f32[256,512]{1,0:T(8,128)S(1)}, f32[256,512]{1,0:T(8,128)}, u32[]{:S(2)}) copy-start(f32[256,512]{1,0:T(8,128)} %get-tuple-element.28) | copy-start | bytes 1572868
  179.6 16.7 %all-to-all-start.8 = ((bf16[4,8,16,512]{3,2,1,0:T(8,128)(2,1)}), bf16[4,8,16,512]{3,2,1,0:T(8,128)(2,1)}, u32[]{:S(2)}, u32[]{:S(2)}) async-start(bf16[4,8,16,512]{3,2,1,0:T(8,128)(2,1)} %copy.125), calls=%async_computation.8 | async-start | bytes 1048576 | tf_op jit(solution)/shard_map/all_to_all | solution.py:102
  183.7 2.4 copy-start.4
  186.1 1.7 copy-start.10
  198.2 14.0 %all-to-all-start.9 = ((bf16[4,8,16,512]{3,2,0,1:T(8,128)(2,1)}), bf16[4,8,16,512]{3,2,0,1:T(8,128)(2,1)S(1)}, u32[]{:S(2)}, u32[]{:S(2)}) async-start(bf16[4,8,16,512]{3,2,0,1:T(8,128)(2,1)} %copy.126), calls=%async_computation.9 | async-start | bytes 1048576 | tf_op jit(solution)/shard_map/all_to_all | solution.py:101
  202.5 182.8 %all-reduce.3.cloned.1.call-start = ((), (), s32[]{:S(2)}) async-start(), calls=%async_computation.12 | async-start | bytes 12582912 | tf_op jit(solution)/shard_map/psum | solution.py:90
  212.5 4.1 %copy-start.12 = (f32[256,512]{1,0:T(8,128)S(1)}, f32[256,512]{1,0:T(8,128)}, u32[]{:S(2)}) copy-start(f32[256,512]{1,0:T(8,128)} %get-tuple-element.26) | copy-start | bytes 1572868
  212.5 4.3 %copy-start.8 = (bf16[2,512,128]{1,2,0:T(8,128)(2,1)S(1)}, bf16[2,512,128]{1,2,0:T(8,128)(2,1)}, u32[]{:S(2)}) copy-start(bf16[2,512,128]{1,2,0:T(8,128)(2,1)} %copy-done.7) | copy-start | bytes 786436
  249.5 13.1 %all-to-all-start.11 = ((bf16[4,8,16,512]{3,2,0,1:T(8,128)(2,1)}), bf16[4,8,16,512]{3,2,0,1:T(8,128)(2,1)S(1)}, u32[]{:S(2)}, u32[]{:S(2)}) async-start(bf16[4,8,16,512]{3,2,0,1:T(8,128)(2,1)} %copy.137), calls=%async_computation.11 | async-start | bytes 1048576 | tf_op jit(solution)/shard_map/all_to_all | solution.py:101
  385.3 2.0 copy-start.5
  385.3 2.2 copy-start.6
  (4 other events, 5.4 us)
Sparse Core Ops, SparseCore 0:
  219.6 165.6 all-reduce.2
where the time goes:
time: 402 us; the launch traced here: 400 us
  waiting for transfers between devices  186 us (46%)
  blocking collectives  72.8 us (18%)
  matrix products  39.5 us (10%)
  local copies, waits for them, and re-layouts  34.6 us (9%)
  starting transfers between devices  32.8 us (8%)
  other arithmetic  19.4 us (5%)
  between operations  14.7 us (4%)
    psum x1, waiting for transfers between devices, per_device(): self_sum, neigh_sum = lax.psum((self_term, neigh_term), ('gx', 'gy'))  118 us
    all_to_all x3, blocking collectives, per_device(): lax.all_to_all(picked, 'gx', split_axis=0, concat_axis=0, tiled=True)  50.6 us
    all_to_all x3, waiting for transfers between devices, per_device(): lax.all_to_all(lax.all_to_all(picked, 'gx', split_axis=0, concat_axis=0,...  25.7 us
    all_to_all x3, waiting for transfers between devices, per_device(): lax.all_to_all(lax.all_to_all(outgoing, 'gx', split_axis=0, concat_axis=0...  23 us
    all_to_all x1, blocking collectives, per_device(): lax.all_to_all(outgoing, 'gx', split_axis=0, concat_axis=0, tiled=True)  22.2 us
    all_to_all x2, waiting for transfers between devices, per_device(): lax.all_to_all(outgoing, 'gx', split_axis=0, concat_axis=0, tiled=True)  19.7 us
    all_to_all x3, starting transfers between devices, per_device(): lax.all_to_all(lax.all_to_all(picked, 'gx', split_axis=0, concat_axis=0,...  12.4 us
    all_to_all x3, starting transfers between devices, per_device(): lax.all_to_all(lax.all_to_all(outgoing, 'gx', split_axis=0, concat_axis=0...  12.1 us
  transfers between devices with their start and end apart: 9, of which 9 were waited for; matrix products, arithmetic and copies ran while one was open for 7% of the time, Pallas kernels for 0%

commit v1 on v0

--- a/solution.py
+++ b/solution.py
@@ -98,12 +98,20 @@
         ).astype(jnp.bfloat16)
         ext_grad = spread_back(upstream, block_val, block_col, ext_tiles, tile)
         outgoing = ext_grad[node_rows:].astype(jnp.bfloat16).reshape(outer, inner, slots, width)
-        arrived = lax.all_to_all(
-            lax.all_to_all(outgoing, "gx", split_axis=0, concat_axis=0, tiled=True),
-            "gy",
-            split_axis=1,
-            concat_axis=1,
-            tiled=True,
+        arrived = jnp.concatenate(
+            lax.all_to_all(
+                jnp.stack(
+                    jnp.split(
+                        lax.all_to_all(outgoing, "gx", split_axis=0, concat_axis=0, tiled=True),
+                        lax.axis_size("gy"),
+                        axis=1,
+                    )
+                ),
+                "gy",
+                0,
+                0,
+            ),
+            axis=1,
         )
         masked = jnp.where(
             live, arrived.reshape(halo_rows, width).astype(jnp.float32), jnp.zeros((), jnp.float32)

time: 402 us -> 430 us (1.070)
  local copies, waits for them, and re-layouts: 34.6 us -> 59.5 us
  blocking collectives: 72.8 us -> 50.6 us
  waiting for transfers between devices: 186 us -> 206 us
  starting transfers between devices: 32.8 us -> 37.1 us
    unnamed x41 -> x66, local copies, waits for them, and re-layouts: 4.99 us -> 31.2 us
    all_to_all x1 -> x0, blocking collectives: 22.2 us -> none  [per_device(): lax.all_to_all(outgoing, 'gx', split_axis=0, concat_axis=0, tiled=True)]
    all_to_all x2 -> x3, waiting for transfers between devices: 19.7 us -> 28.5 us  [per_device(): lax.all_to_all(outgoing, 'gx', split_axis=0, concat_axis=0, tiled=True)]
    psum x1, waiting for transfers between devices: 118 us -> 125 us  [per_device(): self_sum, neigh_sum = lax.psum((self_term, neigh_term), ('gx', 'gy'))]
    all_to_all x3 -> x0, local copies, waits for them, and re-layouts: 4.59 us -> none  [per_device(): lax.all_to_all(outgoing, 'gx', split_axis=0, concat_axis=0, tiled=True)]
    all_to_all x2 -> x3, starting transfers between devices: 8.28 us -> 11.7 us  [per_device(): lax.all_to_all(outgoing, 'gx', split_axis=0, concat_axis=0, tiled=True)]
  transfers between devices with their start and end apart: 9 -> 10, of which waited for: 9 -> 10; matrix products, arithmetic and copies ran while one was open for 7% -> 7% of each run, Pallas kernels for 0% -> 0%
where the time goes in v1:
time: 430 us; the launch traced here: 428 us
  waiting for transfers between devices  206 us (48%)
  local copies, waits for them, and re-layouts  59.5 us (14%)
  blocking collectives  50.6 us (12%)
  matrix products  40.5 us (9%)
  starting transfers between devices  37.1 us (9%)
  other arithmetic  19.5 us (5%)
  between operations  14.7 us (3%)
    psum x1, waiting for transfers between devices, per_device(): self_sum, neigh_sum = lax.psum((self_term, neigh_term), ('gx', 'gy'))  125 us
    all_to_all x3, blocking collectives, per_device(): lax.all_to_all(picked, 'gx', split_axis=0, concat_axis=0, tiled=True)  50.6 us
    unnamed x66, local copies, waits for them, and re-layouts  31.2 us
    all_to_all x3, waiting for transfers between devices, per_device(): lax.all_to_all(outgoing, 'gx', split_axis=0, concat_axis=0, tiled=True)  28.5 us
    all_to_all x3, waiting for transfers between devices, per_device(): lax.all_to_all(jnp.stack(jnp.split(lax.all_to_all(outgoing, 'gx', split_a...  26.7 us
    all_to_all x3, waiting for transfers between devices, per_device(): lax.all_to_all(lax.all_to_all(picked, 'gx', split_axis=0, concat_axis=0,...  25.7 us
    all_to_all x3, starting transfers between devices, per_device(): lax.all_to_all(jnp.stack(jnp.split(lax.all_to_all(outgoing, 'gx', split_a...  13 us
    all_to_all x3, starting transfers between devices, per_device(): lax.all_to_all(lax.all_to_all(picked, 'gx', split_axis=0, concat_axis=0,...  12.4 us
  transfers between devices with their start and end apart: 10, of which 10 were waited for; matrix products, arithmetic and copies ran while one was open for 7% of the time, Pallas kernels for 0%

profile of v1, /device:TPU:0, one launch (start us, length us, event | category | flops | bytes accessed | tf_op | source)
XLA Modules:
  0.0 427.7 jit_solution(13328187796087341361)
XLA Ops:
  12.9 20.8 %all_to_all.60 = bf16[4,8,16,512]{3,2,1,0:T(8,128)(2,1)S(1)} all-to-all(bf16[4,8,16,512]{3,2,1,0:T(8,128)(2,1)S(1)} %bitcast.328), channel_id=1, replica_groups=mesh['gx'=4,'gy'=8] {'gx'}, dimensions={0} | all-to-all | bytes 1048576 | tf_op jit(solution)/shard_map/all_to_all | solution.py:57
  34.5 3.7 all-to-all-start.1
  39.3 8.6 %all-to-all-done.1 = bf16[4,8,16,512]{3,2,0,1:T(8,128)(2,1)S(1)} async-done(((bf16[4,8,16,512]{3,2,0,1:T(8,128)(2,1)}), bf16[4,8,16,512]{3,2,0,1:T(8,128)(2,1)S(1)}, u32[]{:S(2)}, u32[]{:S(2)}) %all-to-all-start.1) | async-done | bytes 524320 | tf_op jit(solution)/shard_map/all_to_all | solution.py:56
  55.7 14.9 %all_to_all.61 = bf16[4,8,16,512]{3,2,1,0:T(8,128)(2,1)S(1)} all-to-all(bf16[4,8,16,512]{3,2,1,0:T(8,128)(2,1)S(1)} %bitcast.329), channel_id=1, replica_groups=mesh['gx'=4,'gy'=8] {'gx'}, dimensions={0} | all-to-all | bytes 1048576 | tf_op jit(solution)/shard_map/all_to_all | solution.py:57
  71.4 4.3 %all-to-all-start.3 = ((bf16[4,8,16,512]{3,2,0,1:T(8,128)(2,1)}), bf16[4,8,16,512]{3,2,0,1:T(8,128)(2,1)S(1)}, u32[]{:S(2)}, u32[]{:S(2)}) async-start(bf16[4,8,16,512]{3,2,0,1:T(8,128)(2,1)} %copy.195), calls=%async_computation.3 | async-start | bytes 1048576 | tf_op jit(solution)/shard_map/all_to_all | solution.py:56
  76.9 8.6 %all-to-all-done.3 = bf16[4,8,16,512]{3,2,0,1:T(8,128)(2,1)S(1)} async-done(((bf16[4,8,16,512]{3,2,0,1:T(8,128)(2,1)}), bf16[4,8,16,512]{3,2,0,1:T(8,128)(2,1)S(1)}, u32[]{:S(2)}, u32[]{:S(2)}) %all-to-all-start.3) | async-done | bytes 524320 | tf_op jit(solution)/shard_map/all_to_all | solution.py:56
  93.2 14.9 %all_to_all.62 = bf16[4,8,16,512]{3,2,1,0:T(8,128)(2,1)S(1)} all-to-all(bf16[4,8,16,512]{3,2,1,0:T(8,128)(2,1)S(1)} %bitcast.327), channel_id=1, replica_groups=mesh['gx'=4,'gy'=8] {'gx'}, dimensions={0} | all-to-all | bytes 1048576 | tf_op jit(solution)/shard_map/all_to_all | solution.py:57
  109.0 4.3 %all-to-all-start.5 = ((bf16[4,8,16,512]{3,2,0,1:T(8,128)(2,1)}), bf16[4,8,16,512]{3,2,0,1:T(8,128)(2,1)S(1)}, u32[]{:S(2)}, u32[]{:S(2)}) async-start(bf16[4,8,16,512]{3,2,0,1:T(8,128)(2,1)} %copy.197), calls=%async_computation.5 | async-start | bytes 1048576 | tf_op jit(solution)/shard_map/all_to_all | solution.py:56
  114.4 8.5 %all-to-all-done.5 = bf16[4,8,16,512]{3,2,0,1:T(8,128)(2,1)S(1)} async-done(((bf16[4,8,16,512]{3,2,0,1:T(8,128)(2,1)}), bf16[4,8,16,512]{3,2,0,1:T(8,128)(2,1)S(1)}, u32[]{:S(2)}, u32[]{:S(2)}) %all-to-all-start.5) | async-done | bytes 524320 | tf_op jit(solution)/shard_map/all_to_all | solution.py:56
  134.2 4.1 all-to-all-start.6
  138.4 12.5 %all-to-all-done.6 = bf16[4,8,16,512]{3,2,1,0:T(8,128)(2,1)} async-done(((bf16[4,8,16,512]{3,2,1,0:T(8,128)(2,1)}), bf16[4,8,16,512]{3,2,1,0:T(8,128)(2,1)}, u32[]{:S(2)}, u32[]{:S(2)}) %all-to-all-start.6) | async-done | bytes 524320 | tf_op jit(solution)/shard_map/all_to_all | solution.py:105
  162.7 4.3 %all-to-all-start.7 = ((bf16[8,4,1,16,512]{4,3,1,2,0:T(8,128)(2,1)}), bf16[8,4,1,16,512]{4,3,1,2,0:T(8,128)(2,1)}, u32[]{:S(2)}, u32[]{:S(2)}) async-start(bf16[8,4,1,16,512]{4,3,1,2,0:T(8,128)(2,1)} %fusion.54), calls=%async_computation.7 | async-start | bytes 1048576 | tf_op jit(solution)/shard_map/all_to_all | solution.py:102
  168.8 8.1 %all-to-all-done.7 = bf16[8,4,1,16,512]{4,3,1,2,0:T(8,128)(2,1)} async-done(((bf16[8,4,1,16,512]{4,3,1,2,0:T(8,128)(2,1)}), bf16[8,4,1,16,512]{4,3,1,2,0:T(8,128)(2,1)}, u32[]{:S(2)}, u32[]{:S(2)}) %all-to-all-start.7) | async-done | bytes 524320 | tf_op jit(solution)/shard_map/all_to_all | solution.py:102
  178.3 4.0 scatter_fusion
  190.3 4.1 all-to-all-start.8
  199.9 7.2 %all-to-all-done.8 = bf16[4,8,16,512]{3,2,1,0:T(8,128)(2,1)} async-done(((bf16[4,8,16,512]{3,2,1,0:T(8,128)(2,1)}), bf16[4,8,16,512]{3,2,1,0:T(8,128)(2,1)}, u32[]{:S(2)}, u32[]{:S(2)}) %all-to-all-start.8) | async-done | bytes 524320 | tf_op jit(solution)/shard_map/all_to_all | solution.py:105
  218.7 4.3 %all-to-all-start.9 = ((bf16[8,4,1,16,512]{4,3,1,2,0:T(8,128)(2,1)}), bf16[8,4,1,16,512]{4,3,1,2,0:T(8,128)(2,1)S(1)}, u32[]{:S(2)}, u32[]{:S(2)}) async-start(bf16[8,4,1,16,512]{4,3,1,2,0:T(8,128)(2,1)} %fusion.46), calls=%async_computation.9 | async-start | bytes 1048576 | tf_op jit(solution)/shard_map/all_to_all | solution.py:102
  225.7 7.0 %all-to-all-done.9 = bf16[8,4,1,16,512]{4,3,1,2,0:T(8,128)(2,1)S(1)} async-done(((bf16[8,4,1,16,512]{4,3,1,2,0:T(8,128)(2,1)}), bf16[8,4,1,16,512]{4,3,1,2,0:T(8,128)(2,1)S(1)}, u32[]{:S(2)}, u32[]{:S(2)}) %all-to-all-start.9) | async-done | bytes 524320 | tf_op jit(solution)/shard_map/all_to_all | solution.py:102
  233.1 4.0 scatter_fusion.1
  252.4 8.8 %all-to-all-done.10 = bf16[4,8,16,512]{3,2,1,0:T(8,128)(2,1)S(1)} async-done(((bf16[4,8,16,512]{3,2,1,0:T(8,128)(2,1)}), bf16[4,8,16,512]{3,2,1,0:T(8,128)(2,1)S(1)}, u32[]{:S(2)}, u32[]{:S(2)}) %all-to-all-start.10) | async-done | bytes 524320 | tf_op jit(solution)/shard_map/all_to_all | solution.py:105
  266.1 4.3 %all-to-all-start.11 = ((bf16[8,4,1,16,512]{4,3,1,2,0:T(8,128)(2,1)}), bf16[8,4,1,16,512]{4,3,1,2,0:T(8,128)(2,1)S(1)}, u32[]{:S(2)}, u32[]{:S(2)}) async-start(bf16[8,4,1,16,512]{4,3,1,2,0:T(8,128)(2,1)} %fusion.38), calls=%async_computation.11 | async-start | bytes 1048576 | tf_op jit(solution)/shard_map/all_to_all | solution.py:102
  272.2 11.6 %all-to-all-done.11 = bf16[8,4,1,16,512]{4,3,1,2,0:T(8,128)(2,1)S(1)} async-done(((bf16[8,4,1,16,512]{4,3,1,2,0:T(8,128)(2,1)}), bf16[8,4,1,16,512]{4,3,1,2,0:T(8,128)(2,1)S(1)}, u32[]{:S(2)}, u32[]{:S(2)}) %all-to-all-start.11) | async-done | bytes 524320 | tf_op jit(solution)/shard_map/all_to_all | solution.py:102
  284.2 3.8 scatter_fusion.2
  288.7 125.0 %all-reduce.3.cloned.1.call-done = (f32[512,512]{0,1:T(8,128)}, f32[512,512]{0,1:T(8,128)}, f32[512,512]{0,1:T(8,128)}, f32[512,512]{0,1:T(8,128)}, f32[512,512]{0,1:T(8,128)}, /*index=5*/f32[512,512]{0,1:T(8,128)}) async-done(((f32[512,512]{0,1:T(8,128)}, f32[512,512]{0,1:T(8,128)}, f32[512,512]{0,1:T(8,128)}, f32[512,512]{0,1:T(8,128)}, f32[512,512]{0,1:T(8,128)}, /*index=5*/f32[512,512]{0,1:T(8,128)}), ...) | async-done | bytes 6291472 | tf_op jit(solution)/shard_map/psum | solution.py:90
  (163 shorter events, 111.1 us)
Async XLA Ops:
  7.2 42.5 %copy-start = (bf16[2,4,128,128]{3,2,1,0:T(8,128)(2,1)S(1)}, bf16[2,4,128,128]{3,2,1,0:T(8,128)(2,1)}, u32[]{:S(2)}) copy-start(bf16[2,4,128,128]{3,2,1,0:T(8,128)(2,1)} %param.14) | copy-start | bytes 786436
  12.9 25.3 %copy-start.1 = (bf16[256,512]{1,0:T(8,128)(2,1)S(1)}, bf16[256,512]{1,0:T(8,128)(2,1)}, u32[]{:S(2)}) copy-start(bf16[256,512]{1,0:T(8,128)(2,1)} %param.10) | copy-start | bytes 786436
  12.9 25.3 %copy-start.2 = (bf16[3,512,512]{2,1,0:T(8,128)(2,1)S(1)}, bf16[3,512,512]{2,1,0:T(8,128)(2,1)}, u32[]{:S(2)}) copy-start(bf16[3,512,512]{2,1,0:T(8,128)(2,1)} %param.12) | copy-start | bytes 4718596
  34.5 13.4 %all-to-all-start.1 = ((bf16[4,8,16,512]{3,2,0,1:T(8,128)(2,1)}), bf16[4,8,16,512]{3,2,0,1:T(8,128)(2,1)S(1)}, u32[]{:S(2)}, u32[]{:S(2)}) async-start(bf16[4,8,16,512]{3,2,0,1:T(8,128)(2,1)} %copy.193), calls=%async_computation.1 | async-start | bytes 1048576 | tf_op jit(solution)/shard_map/all_to_all | solution.py:56
  51.2 2.3 copy-start.10
  71.4 14.0 %all-to-all-start.3 = ((bf16[4,8,16,512]{3,2,0,1:T(8,128)(2,1)}), bf16[4,8,16,512]{3,2,0,1:T(8,128)(2,1)S(1)}, u32[]{:S(2)}, u32[]{:S(2)}) async-start(bf16[4,8,16,512]{3,2,0,1:T(8,128)(2,1)} %copy.195), calls=%async_computation.3 | async-start | bytes 1048576 | tf_op jit(solution)/shard_map/all_to_all | solution.py:56
  87.2 1.6 copy-start.17
  88.8 2.3 copy-start.11
  93.2 20.1 %copy-start.19 = (s32[2,4]{1,0:T(2,128)S(1)}, s32[2,4]{1,0:T(2,128)}, u32[]{:S(2)}) copy-start(s32[2,4]{1,0:T(2,128)} %param.15) | copy-start | bytes 100
  109.0 14.0 %all-to-all-start.5 = ((bf16[4,8,16,512]{3,2,0,1:T(8,128)(2,1)}), bf16[4,8,16,512]{3,2,0,1:T(8,128)(2,1)S(1)}, u32[]{:S(2)}, u32[]{:S(2)}) async-start(bf16[4,8,16,512]{3,2,0,1:T(8,128)(2,1)} %copy.197), calls=%async_computation.5 | async-start | bytes 1048576 | tf_op jit(solution)/shard_map/all_to_all | solution.py:56
  124.0 2.3 copy-start.13
  126.3 41.1 %copy-start.3 = (bf16[256,512]{1,0:T(8,128)(2,1)}, bf16[256,512]{1,0:T(8,128)(2,1)S(1)}, u32[]{:S(2)}) copy-start(bf16[256,512]{1,0:T(8,128)(2,1)S(1)} %multiply_convert_fusion.8) | copy-start | bytes 786436
  134.2 16.7 %all-to-all-start.6 = ((bf16[4,8,16,512]{3,2,1,0:T(8,128)(2,1)}), bf16[4,8,16,512]{3,2,1,0:T(8,128)(2,1)}, u32[]{:S(2)}, u32[]{:S(2)}) async-start(bf16[4,8,16,512]{3,2,1,0:T(8,128)(2,1)} %copy.203), calls=%async_computation.6 | async-start | bytes 1048576 | tf_op jit(solution)/shard_map/all_to_all | solution.py:105
  162.7 14.1 %all-to-all-start.7 = ((bf16[8,4,1,16,512]{4,3,1,2,0:T(8,128)(2,1)}), bf16[8,4,1,16,512]{4,3,1,2,0:T(8,128)(2,1)}, u32[]{:S(2)}, u32[]{:S(2)}) async-start(bf16[8,4,1,16,512]{4,3,1,2,0:T(8,128)(2,1)} %fusion.54), calls=%async_computation.7 | async-start | bytes 1048576 | tf_op jit(solution)/shard_map/all_to_all | solution.py:102
  178.3 4.0 copy-start.15
  190.3 16.7 %all-to-all-start.8 = ((bf16[4,8,16,512]{3,2,1,0:T(8,128)(2,1)}), bf16[4,8,16,512]{3,2,1,0:T(8,128)(2,1)}, u32[]{:S(2)}, u32[]{:S(2)}) async-start(bf16[4,8,16,512]{3,2,1,0:T(8,128)(2,1)} %copy.215), calls=%async_computation.8 | async-start | bytes 1048576 | tf_op jit(solution)/shard_map/all_to_all | solution.py:105
  194.5 2.4 copy-start.4
  196.9 1.7 copy-start.12
  218.7 14.0 %all-to-all-start.9 = ((bf16[8,4,1,16,512]{4,3,1,2,0:T(8,128)(2,1)}), bf16[8,4,1,16,512]{4,3,1,2,0:T(8,128)(2,1)S(1)}, u32[]{:S(2)}, u32[]{:S(2)}) async-start(bf16[8,4,1,16,512]{4,3,1,2,0:T(8,128)(2,1)} %fusion.46), calls=%async_computation.9 | async-start | bytes 1048576 | tf_op jit(solution)/shard_map/all_to_all | solution.py:102
  233.1 4.0 copy-start.14
  245.2 16.0 %all-to-all-start.10 = ((bf16[4,8,16,512]{3,2,1,0:T(8,128)(2,1)}), bf16[4,8,16,512]{3,2,1,0:T(8,128)(2,1)S(1)}, u32[]{:S(2)}, u32[]{:S(2)}) async-start(bf16[4,8,16,512]{3,2,1,0:T(8,128)(2,1)} %copy.232), calls=%async_computation.10 | async-start | bytes 1048576 | tf_op jit(solution)/shard_map/all_to_all | solution.py:105
  248.7 165.0 %all-reduce.3.cloned.1.call-start = ((), (), s32[]{:S(2)}) async-start(), calls=%async_computation.12 | async-start | bytes 12582912 | tf_op jit(solution)/shard_map/psum | solution.py:90
  266.1 17.6 %all-to-all-start.11 = ((bf16[8,4,1,16,512]{4,3,1,2,0:T(8,128)(2,1)}), bf16[8,4,1,16,512]{4,3,1,2,0:T(8,128)(2,1)S(1)}, u32[]{:S(2)}, u32[]{:S(2)}) async-start(bf16[8,4,1,16,512]{4,3,1,2,0:T(8,128)(2,1)} %fusion.38), calls=%async_computation.11 | async-start | bytes 1048576 | tf_op jit(solution)/shard_map/all_to_all | solution.py:102
  413.7 1.9 copy-start.8
  (7 other events, 9.6 us)
Sparse Core Ops, SparseCore 0:
  256.5 157.1 all-reduce.2
